TPU v7x, 32 devices: a whole 2x2x4 slice. The times are simulated.
32 devices in a mesh: groups: 1, orient: 8 (over z, core), cls: 4 (over y, x).
Axes of the slice: x: 2, y: 2, z: 4, core: 2. Of those that a mesh axis runs over, the one named last changes fastest.
Arguments:
- particles: bfloat16 [384, 33024], P(('groups', 'orient', 'cls')), may hold values from -300 to 300
- projections: bfloat16 [8, 8, 33024], P('cls', 'orient')
- ctf: bfloat16 [8, 16512], replicated, may hold values from -1 to 1
- defocus_group: int32 [384], P(('groups', 'orient', 'cls')), may hold values from 0 to 7
- offsets: int32 [384, 2], P(('groups', 'orient', 'cls')), may hold values from -8 to 8
- routes: int32 [384, 4], P(('groups', 'orient', 'cls')), may hold values from 0 to 7, all different within a row; in each aligned block of 12 rows (0 to 11, 12 to 23, ...) at most 6 rows name the same one
Outputs:
- log_evidence: float32 [384], P(('groups', 'orient', 'cls'))
- data_sum: bfloat16 [8, 8, 33024], P(('groups', 'cls'), 'orient')
Inputs may be any that keep to these rules, and one draw needn't show every extreme that they name: `routes`: the 4 blocks of a particle differ; among the particles of one device no block is listed more than 6 times, and some block is listed exactly 6 times.
All inputs are finite; a program needn't handle non-finite values.
Results may differ from a plain program's by a relative error of at most 0.01.
The roundings to bfloat16 on the way count: a program that leaves them out, or rounds other values in their place, can miss the bound.
Values may be sent and summed in bfloat16 or wider, within the bound.
No kernel may reach another device: no remote copies, remote signals or barrier semaphores. Data moves between devices by JAX's collectives and lax.ppermute only.
A program may use at most 64 MiB of HBM per device.

v0:
```python
import math
import jax
import jax.numpy as jnp
import numpy as np
from jax import lax
from jax.sharding import PartitionSpec as P

KX = 86
KY = 192
BOX = 256
two_pi = 2.0 * math.pi
highest = lax.Precision.HIGHEST
local_across = np.array([0, 1, -1, 0, 0], dtype=np.int32)
local_down = np.array([0, 0, 0, 1, -1], dtype=np.int32)


def frequencies():
    column = jnp.arange(KX * KY, dtype=jnp.int32)
    return (column // KY, column % KY - KY // 2)


def rotation(shift_across, shift_down, freq_across, freq_down):
    turns = jnp.mod(freq_across * shift_across + freq_down * shift_down, BOX)
    angle = turns.astype(jnp.float32) * (two_pi / BOX)
    return (jnp.cos(angle), jnp.sin(angle))


def combine_stats(peaks, masses):
    top_value = jnp.max(peaks, axis=-1, keepdims=True)
    return top_value[..., 0] + jnp.log(jnp.sum(masses * jnp.exp(peaks - top_value), axis=-1))


def align_images(images, ctf_rows, shifts, freq_across, freq_down, pixel_count):
    real_part = images[:, :pixel_count].astype(jnp.float32)
    imag_part = images[:, pixel_count:].astype(jnp.float32)
    cos_base, sin_base = rotation(
        shifts[:, 0:1], shifts[:, 1:2], freq_across[None, :], freq_down[None, :]
    )
    first = (real_part * cos_base + imag_part * sin_base) * ctf_rows
    second = (imag_part * cos_base - real_part * sin_base) * ctf_rows
    return jnp.concatenate([first, second], axis=1).astype(jnp.bfloat16)


def spread_phase(table, ndim_rest):
    return table.reshape((table.shape[0],) + (1,) * ndim_rest + (table.shape[1],))


def turn_refs(ref_block, cos_shift, sin_shift, pixel_count):
    real_ref = ref_block[..., :pixel_count].astype(jnp.float32)
    imag_ref = ref_block[..., pixel_count:].astype(jnp.float32)
    cos_wide = spread_phase(cos_shift, real_ref.ndim - 1)
    sin_wide = spread_phase(sin_shift, real_ref.ndim - 1)
    first = real_ref[None] * cos_wide - imag_ref[None] * sin_wide
    second = real_ref[None] * sin_wide + imag_ref[None] * cos_wide
    turned = jnp.concatenate([first, second], axis=-1).astype(jnp.bfloat16)
    return (turned, real_ref * real_ref + imag_ref * imag_ref)


def back_rotate(summed, cos_shift, sin_shift, pixel_count):
    cos_wide = spread_phase(cos_shift, summed.ndim - 2)
    sin_wide = spread_phase(sin_shift, summed.ndim - 2)
    real_sum = summed[..., :pixel_count]
    imag_sum = summed[..., pixel_count:]
    first = jnp.sum(real_sum * cos_wide + imag_sum * sin_wide, axis=0)
    second = jnp.sum(imag_sum * cos_wide - real_sum * sin_wide, axis=0)
    return jnp.concatenate([first, second], axis=-1)


def slot_places(route_rows, orient_size):
    targets = route_rows.reshape(-1)
    onehot = (targets[:, None] == jnp.arange(orient_size, dtype=jnp.int32)[None, :]).astype(
        jnp.int32
    )
    before = jnp.cumsum(onehot, axis=0) - onehot
    return (targets, jnp.sum(before * onehot, axis=1))


def per_device(particles, projections, ctf, defocus_group, offsets, routes):
    pixel_count = KX * KY
    own_count = particles.shape[0]
    route_count = routes.shape[1]
    class_local = projections.shape[0]
    directions = projections.shape[1]
    group_count = ctf.shape[0]
    orient_size = lax.axis_size("orient")
    capacity = max(2, (own_count * route_count + orient_size - 1) // orient_size)
    total_slots = orient_size * capacity
    freq_across, freq_down = frequencies()
    ctf_table = ctf.astype(jnp.float32)
    group_onehot = (
        defocus_group[:, None] == jnp.arange(group_count, dtype=jnp.int32)[None, :]
    ).astype(jnp.float32)
    ctf_rows = jnp.dot(group_onehot, ctf_table, precision=highest)
    aligned = align_images(particles, ctf_rows, offsets, freq_across, freq_down, pixel_count)
    targets, orders = slot_places(routes, orient_size)
    slot_ids = targets * capacity + orders
    matches = (slot_ids[None, :] == jnp.arange(total_slots, dtype=jnp.int32)[:, None]).astype(
        jnp.int32
    )
    picked = jnp.sum(matches.reshape(total_slots, own_count, route_count), axis=2)
    send_images = jnp.dot(picked.astype(jnp.bfloat16), aligned, preferred_element_type=jnp.float32)
    send_images = send_images.astype(jnp.bfloat16).reshape(orient_size, capacity, 2 * pixel_count)
    send_codes = jnp.sum(picked * (defocus_group + 1)[None, :], axis=1).reshape(
        orient_size, capacity
    )
    tiles, codes = (
        lax.all_to_all(send_images, "orient", split_axis=0, concat_axis=0, tiled=True),
        lax.all_to_all(send_codes, "orient", split_axis=0, concat_axis=0, tiled=True),
    )
    rows_in = tiles.reshape(total_slots, 2 * pixel_count)
    codes_in = codes.reshape(total_slots)
    slot_groups = (
        codes_in[:, None] - 1 == jnp.arange(group_count, dtype=jnp.int32)[None, :]
    ).astype(jnp.float32)
    occupied = codes_in > 0
    cos_shift, sin_shift = rotation(
        jnp.asarray(local_across, dtype=jnp.int32)[:, None],
        jnp.asarray(local_down, dtype=jnp.int32)[:, None],
        freq_across[None, :],
        freq_down[None, :],
    )
    shift_total = cos_shift.shape[0]
    ctf_square = ctf_table * ctf_table
    ref_piece = lax.all_gather(projections, "cls", axis=0, tiled=True)
    piece_rows = ref_piece.shape[0]
    group_size = 2
    grouped = ref_piece.reshape(piece_rows // group_size, group_size, directions, 2 * pixel_count)

    def one_group(ref_block):
        turned, magnitude = turn_refs(ref_block, cos_shift, sin_shift, pixel_count)
        products = lax.dot_general(
            rows_in,
            turned.reshape(-1, 2 * pixel_count),
            (((1,), (1,)), ((), ())),
            preferred_element_type=jnp.float32,
        )
        energy = lax.dot_general(
            ctf_square,
            magnitude.reshape(group_size * directions, pixel_count),
            (((1,), (1,)), ((), ())),
            precision=highest,
        )
        slot_energy = jnp.dot(slot_groups, energy, precision=highest).reshape(
            total_slots, 1, group_size, directions
        )
        return (
            products.reshape(total_slots, shift_total, group_size, directions) - 0.5 * slot_energy
        )

    stacked = lax.map(one_group, grouped)
    scores = jnp.transpose(stacked, (1, 2, 0, 3, 4)).reshape(
        total_slots, shift_total, piece_rows, directions
    )
    slot_peak = jnp.max(scores, axis=(1, 2, 3))
    slot_mass = jnp.sum(jnp.exp(scores - slot_peak[:, None, None, None]), axis=(1, 2, 3))
    back_peak, back_mass = (
        lax.all_to_all(
            slot_peak.reshape(orient_size, capacity),
            "orient",
            split_axis=0,
            concat_axis=0,
            tiled=True,
        ),
        lax.all_to_all(
            slot_mass.reshape(orient_size, capacity),
            "orient",
            split_axis=0,
            concat_axis=0,
            tiled=True,
        ),
    )
    match_table = matches.astype(jnp.float32)
    entry_peak = jnp.dot(back_peak.reshape(-1), match_table, precision=highest).reshape(
        own_count, route_count
    )
    entry_mass = jnp.dot(back_mass.reshape(-1), match_table, precision=highest).reshape(
        own_count, route_count
    )
    log_evidence = combine_stats(entry_peak, entry_mass)
    slot_value = jnp.dot(picked.astype(jnp.float32), log_evidence, precision=highest).reshape(
        orient_size, capacity
    )
    evidence_in = lax.all_to_all(
        slot_value, "orient", split_axis=0, concat_axis=0, tiled=True
    ).reshape(total_slots)
    live = occupied[:, None, None, None]
    exponent = jnp.where(live, scores - evidence_in[:, None, None, None], 0.0)
    weights = jnp.where(live, jnp.exp(exponent), 0.0).astype(jnp.bfloat16)
    class_group_size = 2

    def one_group(group_index):
        weight_part = lax.dynamic_slice_in_dim(
            weights, group_index * class_group_size, class_group_size, 2
        )
        summed = lax.dot_general(
            weight_part.reshape(total_slots, -1),
            rows_in,
            (((0,), (0,)), ((), ())),
            preferred_element_type=jnp.float32,
        )
        summed = summed.reshape(shift_total, class_group_size, directions, 2 * pixel_count)
        return back_rotate(summed, cos_shift, sin_shift, pixel_count)

    results = lax.map(
        one_group,
        jnp.arange(class_local * lax.axis_size("cls") // class_group_size, dtype=jnp.int32),
    )
    data_sum = lax.psum_scatter(
        results.reshape(class_local * lax.axis_size("cls"), directions, 2 * pixel_count).astype(
            jnp.bfloat16
        ),
        "cls",
        scatter_dimension=0,
        tiled=True,
    )
    return (log_evidence, data_sum)


def solution(mesh):
    placed = (
        P(("groups", "orient", "cls"), None),
        P("cls", "orient", None),
        P(),
        P(("groups", "orient", "cls")),
        P(("groups", "orient", "cls"), None),
        P(("groups", "orient", "cls"), None),
    )
    return jax.shard_map(
        per_device,
        mesh=mesh,
        in_specs=placed,
        out_specs=(P(("groups", "orient", "cls")), P(("groups", "cls"), "orient", None)),
        check_vma=False,
    )
```

profile of v0, /device:TPU:0, one launch (start us, length us, event | category | flops | bytes accessed | tf_op | source)
XLA Modules:
  0.0 305.0 jit_solution(8616529737925251293)
XLA Ops:
  10.0 6.4 %all-to-all-start.1 = ((s32[8,1,6]{2,1,0:T(1,128)}), s32[8,1,6]{2,1,0:T(1,128)S(1)}, u32[]{:S(2)}, u32[]{:S(2)}) async-start(s32[8,1,6]{2,1,0:T(1,128)} %bitcast.3), calls=%async_computation.1 | async-start | bytes 8192 | tf_op jit(solution)/shard_map/all_to_all | solution.py:108
  17.8 6.1 %fusion.38 = (bf16[12,16512]{1,0:T(8,128)(2,1)S(1)}, bf16[12,16512]{1,0:T(8,128)(2,1)S(1)}) fusion(s32[12]{0:T(128)S(1)} %get-tuple-element.313, s32[16512]{0:T(1024)} %get-tuple-element.493, s32[12]{0:T(128)S(1)} %get-tuple-element.312, s32[16512]{0:T(1024)} %get-tuple-element.491, bf16[12,33024]{1,0:T(8,128)(2,1)} %param.12, bf16[8,16512]{1,0:T(8,128)(2,1)} %param.14, ...), kind=kOutput, calls=%fused_computation.63 | convolution fusion | flops 8718432 | bytes 1981584 | tf_op jit(solution)/shard_map/dot_general | solution.py:93
  24.9 2.6 reshape.281
  27.5 5.2 %all-to-all-start = ((bf16[8,6,33024]{2,1,0:T(8,128)(2,1)}), bf16[8,6,33024]{2,1,0:T(8,128)(2,1)}, u32[]{:S(2)}, u32[]{:S(2)}) async-start(bf16[8,6,33024]{2,1,0:T(8,128)(2,1)} %reshape.281), calls=%async_computation | async-start | bytes 8454144 | tf_op jit(solution)/shard_map/all_to_all | solution.py:107
  33.0 15.3 %all_gather.3 = bf16[8,1,33024]{2,1,0:T(2,128)(2,1)S(1)} all-gather(bf16[2,1,33024]{2,1,0:T(2,128)(2,1)S(1)} %copy.39), channel_id=1, replica_groups=mesh['groups'=1,'orient'=8,'cls'=4] {'cls'}, dimensions={0}, use_global_device_ids=true | all-gather | bytes 660480 | tf_op jit(solution)/shard_map/all_gather | solution.py:124
  48.2 3.2 %reduce.6 = bf16[8,33024]{1,0:T(8,128)(2,1)S(1)} reduce(bf16[8,1,33024]{2,1,0:T(2,128)(2,1)S(1)} %all_gather.3, bf16[]{:T(256)} %constant.106), dimensions={1}, to_apply=%all_gather.3.reduce_sub_computation | reduce | bytes 1056770 | tf_op jit(solution)/shard_map/all_gather | solution.py:124
  51.4 1.0 reshape.280
  53.4 74.1 %all-to-all-done = bf16[8,6,33024]{2,1,0:T(8,128)(2,1)} async-done(((bf16[8,6,33024]{2,1,0:T(8,128)(2,1)}), bf16[8,6,33024]{2,1,0:T(8,128)(2,1)}, u32[]{:S(2)}, u32[]{:S(2)}) %all-to-all-start) | async-done | bytes 3170336 | tf_op jit(solution)/shard_map/all_to_all | solution.py:107
  127.5 2.8 reshape.282
  130.4 57.9 %while.24 = (s32[]{:T(128)}, f32[4,48,5,2,1]{1,3,2,4,0:T(2,128)S(1)}, bf16[4,2,1,33024]{3,1,2,0:T(2,128)(2,1)}, bf16[48,33024]{1,0:T(8,128)(2,1)S(1)}, f32[8,165...) while((s32[]{:T(128)}, ...), condition=%wide.region_5.6_spmd.clone.clone, body=%wide.region_4.5_spmd.clone.clone.sunk | while | flops 39077952 | bytes 9925141 | solution.py:150
  130.4 3.1 %fusion.95 = (f32[5,16512]{1,0:T(8,128)S(1)}, f32[5,16512]{1,0:T(8,128)S(1)}) fusion(s32[5]{0:T(128)S(1)} %get-tuple-element.481, s32[16512]{0:T(1024)} %get-tuple-element.482, s32[5]{0:T(128)S(1)} %get-tuple-element.479, s32[16512]{0:T(1024)} %get-tuple-element.480), kind=kLoop, calls=%fused_computation.20.clone.1 | loop fusion | flops 1320960 | bytes 792616 | tf_op jit(solution)/shard_map/cos | solution.py:25
  135.1 1.4 subtract_convert_fusion.2
  136.5 2.3 add.652
  138.8 1.3 sub.142
  140.1 2.1 convolution_bitcast_fusion.5
  142.3 2.3 fusion.96
  144.9 3.1 %fusion.95 = (f32[5,16512]{1,0:T(8,128)S(1)}, f32[5,16512]{1,0:T(8,128)S(1)}) fusion(s32[5]{0:T(128)S(1)} %get-tuple-element.481, s32[16512]{0:T(1024)} %get-tuple-element.482, s32[5]{0:T(128)S(1)} %get-tuple-element.479, s32[16512]{0:T(1024)} %get-tuple-element.480), kind=kLoop, calls=%fused_computation.20.clone.1 | loop fusion | flops 1320960 | bytes 792616 | tf_op jit(solution)/shard_map/cos | solution.py:25
  149.6 1.4 subtract_convert_fusion.2
  151.0 2.3 add.652
  153.3 1.3 sub.142
  154.6 2.1 convolution_bitcast_fusion.5
  156.8 2.3 fusion.96
  159.4 3.1 %fusion.95 = (f32[5,16512]{1,0:T(8,128)S(1)}, f32[5,16512]{1,0:T(8,128)S(1)}) fusion(s32[5]{0:T(128)S(1)} %get-tuple-element.481, s32[16512]{0:T(1024)} %get-tuple-element.482, s32[5]{0:T(128)S(1)} %get-tuple-element.479, s32[16512]{0:T(1024)} %get-tuple-element.480), kind=kLoop, calls=%fused_computation.20.clone.1 | loop fusion | flops 1320960 | bytes 792616 | tf_op jit(solution)/shard_map/cos | solution.py:25
  164.1 1.4 subtract_convert_fusion.2
  165.5 2.3 add.652
  167.8 1.3 sub.142
  169.1 2.1 convolution_bitcast_fusion.5
  171.3 2.3 fusion.96
  173.8 3.1 %fusion.95 = (f32[5,16512]{1,0:T(8,128)S(1)}, f32[5,16512]{1,0:T(8,128)S(1)}) fusion(s32[5]{0:T(128)S(1)} %get-tuple-element.481, s32[16512]{0:T(1024)} %get-tuple-element.482, s32[5]{0:T(128)S(1)} %get-tuple-element.479, s32[16512]{0:T(1024)} %get-tuple-element.480), kind=kLoop, calls=%fused_computation.20.clone.1 | loop fusion | flops 1320960 | bytes 792616 | tf_op jit(solution)/shard_map/cos | solution.py:25
  178.6 1.4 subtract_convert_fusion.2
  180.0 2.3 add.652
  182.3 1.3 sub.142
  183.6 2.1 convolution_bitcast_fusion.5
  185.8 2.3 fusion.96
  189.1 3.3 %all-to-all-start.3 = ((f32[8,1,6]{2,1,0:T(1,128)}), f32[8,1,6]{2,1,0:T(1,128)S(1)}, u32[]{:S(2)}, u32[]{:S(2)}) async-start(f32[8,1,6]{2,1,0:T(1,128)} %bitcast.8), calls=%async_computation.3 | async-start | bytes 8192 | tf_op jit(solution)/shard_map/all_to_all | solution.py:164
  193.2 4.7 %all-to-all-done.3 = f32[8,1,6]{2,1,0:T(1,128)S(1)} async-done(((f32[8,1,6]{2,1,0:T(1,128)}), f32[8,1,6]{2,1,0:T(1,128)S(1)}, u32[]{:S(2)}, u32[]{:S(2)}) %all-to-all-start.3) | async-done | bytes 224 | tf_op jit(solution)/shard_map/all_to_all | solution.py:164
  197.9 3.3 %all-to-all-start.2 = ((f32[8,1,6]{2,1,0:T(1,128)}), f32[8,1,6]{2,1,0:T(1,128)S(1)}, u32[]{:S(2)}, u32[]{:S(2)}) async-start(f32[8,1,6]{2,1,0:T(1,128)} %bitcast.4), calls=%async_computation.2 | async-start | bytes 8192 | tf_op jit(solution)/shard_map/all_to_all | solution.py:157
  202.5 4.2 %all-to-all-done.2 = f32[8,1,6]{2,1,0:T(1,128)S(1)} async-done(((f32[8,1,6]{2,1,0:T(1,128)}), f32[8,1,6]{2,1,0:T(1,128)S(1)}, u32[]{:S(2)}, u32[]{:S(2)}) %all-to-all-start.2) | async-done | bytes 224 | tf_op jit(solution)/shard_map/all_to_all | solution.py:157
  209.0 3.3 %all-to-all-start.4 = ((f32[8,1,6]{2,1,0:T(1,128)}), f32[8,1,6]{2,1,0:T(1,128)S(1)}, u32[]{:S(2)}, u32[]{:S(2)}) async-start(f32[8,1,6]{2,1,0:T(1,128)} %bitcast.13), calls=%async_computation.4 | async-start | bytes 8192 | tf_op jit(solution)/shard_map/all_to_all | solution.py:183
  212.7 5.0 %all-to-all-done.4 = f32[8,1,6]{2,1,0:T(1,128)S(1)} async-done(((f32[8,1,6]{2,1,0:T(1,128)}), f32[8,1,6]{2,1,0:T(1,128)S(1)}, u32[]{:S(2)}, u32[]{:S(2)}) %all-to-all-start.4) | async-done | bytes 224 | tf_op jit(solution)/shard_map/all_to_all | solution.py:183
  218.6 28.0 %while.25 = (s32[]{:T(128)}, bf16[4,2,1,33024]{3,2,1,0:T(2,128)(2,1)}, s32[4]{0:T(128)S(1)}, bf16[48,5,8,1]{0,2,1,3:T(8,128)(2,1)S(1)}, bf16[48,33024]{1,0:T(8,1...) while((s32[]{:T(128)}, ...), condition=%wide.region_13.14_spmd.clone.clone, body=%wide.region_10.13_spmd.clone.clone.sunk | while | flops 34543108 | bytes 8065315 | solution.py:204
  220.4 3.1 %fusion.100 = (f32[5,16512]{1,0:T(8,128)S(1)}, f32[5,16512]{1,0:T(8,128)S(1)}) fusion(s32[5]{0:T(128)S(1)} %get-tuple-element.518, s32[16512]{0:T(1024)} %get-tuple-element.519, s32[5]{0:T(128)S(1)} %get-tuple-element.516, s32[16512]{0:T(1024)} %get-tuple-element.517), kind=kLoop, calls=%fused_computation.47.clone.1 | loop fusion | flops 1320960 | bytes 792616 | tf_op jit(solution)/shard_map/cos | solution.py:25
  227.4 3.1 %fusion.100 = (f32[5,16512]{1,0:T(8,128)S(1)}, f32[5,16512]{1,0:T(8,128)S(1)}) fusion(s32[5]{0:T(128)S(1)} %get-tuple-element.518, s32[16512]{0:T(1024)} %get-tuple-element.519, s32[5]{0:T(128)S(1)} %get-tuple-element.516, s32[16512]{0:T(1024)} %get-tuple-element.517), kind=kLoop, calls=%fused_computation.47.clone.1 | loop fusion | flops 1320960 | bytes 792616 | tf_op jit(solution)/shard_map/cos | solution.py:25
  234.4 3.1 %fusion.100 = (f32[5,16512]{1,0:T(8,128)S(1)}, f32[5,16512]{1,0:T(8,128)S(1)}) fusion(s32[5]{0:T(128)S(1)} %get-tuple-element.518, s32[16512]{0:T(1024)} %get-tuple-element.519, s32[5]{0:T(128)S(1)} %get-tuple-element.516, s32[16512]{0:T(1024)} %get-tuple-element.517), kind=kLoop, calls=%fused_computation.47.clone.1 | loop fusion | flops 1320960 | bytes 792616 | tf_op jit(solution)/shard_map/cos | solution.py:25
  241.4 3.1 %fusion.100 = (f32[5,16512]{1,0:T(8,128)S(1)}, f32[5,16512]{1,0:T(8,128)S(1)}) fusion(s32[5]{0:T(128)S(1)} %get-tuple-element.518, s32[16512]{0:T(1024)} %get-tuple-element.519, s32[5]{0:T(128)S(1)} %get-tuple-element.516, s32[16512]{0:T(1024)} %get-tuple-element.517), kind=kLoop, calls=%fused_computation.47.clone.1 | loop fusion | flops 1320960 | bytes 792616 | tf_op jit(solution)/shard_map/cos | solution.py:25
  246.6 4.8 %convert_reduce_fusion = bf16[4,2,33024]{2,1,0:T(2,128)(2,1)S(1)} fusion(bf16[4,2,1,33024]{3,2,1,0:T(2,128)(2,1)} %get-tuple-element.82), kind=kLoop, calls=%fused_computation.73 | loop fusion | bytes 1056768 | tf_op jit(solution)/shard_map/convert_element_type | solution.py:209
  253.7 42.7 %all-reduce.3.cloned.1.call-done = bf16[8,1,33024]{2,0,1:T(8,128)(2,1)} async-done(((bf16[8,1,33024]{2,0,1:T(8,128)(2,1)}), bf16[8,1,33024]{2,0,1:T(8,128)(2,1)}) %all-reduce.3.cloned.1.call-update) | async-done | bytes 528400
  296.4 1.8 constant_dynamic-slice_fusion.1
  (133 shorter events, 34.9 us)
Async XLA Ops:
  10.0 17.5 %all-to-all-start.1 = ((s32[8,1,6]{2,1,0:T(1,128)}), s32[8,1,6]{2,1,0:T(1,128)S(1)}, u32[]{:S(2)}, u32[]{:S(2)}) async-start(s32[8,1,6]{2,1,0:T(1,128)} %bitcast.3), calls=%async_computation.1 | async-start | bytes 8192 | tf_op jit(solution)/shard_map/all_to_all | solution.py:108
  27.5 5.2 %copy-start.3 = (bf16[2,1,33024]{2,0,1:T(2,128)(2,1)S(1)}, bf16[2,1,33024]{2,0,1:T(2,128)(2,1)}, u32[]{:S(2)}) copy-start(bf16[2,1,33024]{2,0,1:T(2,128)(2,1)} %param.13) | copy-start | bytes 396292
  27.5 100.0 %all-to-all-start = ((bf16[8,6,33024]{2,1,0:T(8,128)(2,1)}), bf16[8,6,33024]{2,1,0:T(8,128)(2,1)}, u32[]{:S(2)}, u32[]{:S(2)}) async-start(bf16[8,6,33024]{2,1,0:T(8,128)(2,1)} %reshape.281), calls=%async_computation | async-start | bytes 8454144 | tf_op jit(solution)/shard_map/all_to_all | solution.py:107
  48.2 4.2 %copy-start.2 = (bf16[8,16512]{1,0:T(8,128)(2,1)S(1)}, bf16[8,16512]{1,0:T(8,128)(2,1)}, u32[]{:S(2)}) copy-start(bf16[8,16512]{1,0:T(8,128)(2,1)} %param.14) | copy-start | bytes 792580
  53.4 77.0 %copy-start.4 = (s32[5]{0:T(128)S(1)}, s32[5]{0:T(128)}, u32[]{:S(2)}) copy-start(s32[5]{0:T(128)} %constant.95.clone) | copy-start | bytes 64
  53.4 77.0 %copy-start.5 = (s32[5]{0:T(128)S(1)}, s32[5]{0:T(128)}, u32[]{:S(2)}) copy-start(s32[5]{0:T(128)} %constant.96.clone) | copy-start | bytes 64
  134.5 0.7 copy-start
  140.1 2.2 copy-start.1
  149.0 0.7 copy-start
  154.6 2.2 copy-start.1
  163.5 0.7 copy-start
  169.1 2.2 copy-start.1
  177.9 0.7 copy-start
  183.6 2.2 copy-start.1
  189.1 8.9 %all-to-all-start.3 = ((f32[8,1,6]{2,1,0:T(1,128)}), f32[8,1,6]{2,1,0:T(1,128)S(1)}, u32[]{:S(2)}, u32[]{:S(2)}) async-start(f32[8,1,6]{2,1,0:T(1,128)} %bitcast.8), calls=%async_computation.3 | async-start | bytes 8192 | tf_op jit(solution)/shard_map/all_to_all | solution.py:164
  197.9 8.8 %all-to-all-start.2 = ((f32[8,1,6]{2,1,0:T(1,128)}), f32[8,1,6]{2,1,0:T(1,128)S(1)}, u32[]{:S(2)}, u32[]{:S(2)}) async-start(f32[8,1,6]{2,1,0:T(1,128)} %bitcast.4), calls=%async_computation.2 | async-start | bytes 8192 | tf_op jit(solution)/shard_map/all_to_all | solution.py:157
  208.2 10.4 %copy-start.6 = (f32[12]{0:T(128)}, f32[12]{0:T(128)S(1)}, u32[]{:S(2)}) copy-start(f32[12]{0:T(128)S(1)} %log_add_fusion) | copy-start | bytes 148
  209.0 8.8 %all-to-all-start.4 = ((f32[8,1,6]{2,1,0:T(1,128)}), f32[8,1,6]{2,1,0:T(1,128)S(1)}, u32[]{:S(2)}, u32[]{:S(2)}) async-start(f32[8,1,6]{2,1,0:T(1,128)} %bitcast.13), calls=%async_computation.4 | async-start | bytes 8192 | tf_op jit(solution)/shard_map/all_to_all | solution.py:183
  212.3 84.0 %all-reduce.3.cloned.1.call-start = ((), (), s32[]{:S(2)}) async-start(), calls=%async_computation.5 | async-start | bytes 1056768
  251.4 1.1 copy-start.7
Sparse Core Ops, SparseCore 0:
  252.5 43.7 all-reduce.2
where the time goes:
time: 307 us; the launch traced here: 305 us
  waiting for transfers between devices  131 us (43%)
  other arithmetic  46.6 us (15%)
  local copies, waits for them, and re-layouts  44 us (14%)
  matrix products  28.7 us (9%)
  starting transfers between devices  21.8 us (7%)
  blocking collectives  15.3 us (5%)
  between operations  14.9 us (5%)
    all_to_all x1, waiting for transfers between devices, per_device(): lax.all_to_all(send_images, 'orient', split_axis=0, concat_axis=0, tiled=...  74.1 us
    unnamed x2, waiting for transfers between devices  42.7 us
    cos x8, other arithmetic, rotation(): return (jnp.cos(angle), jnp.sin(angle))  24.6 us
    all_gather x1, blocking collectives, per_device(): ref_piece = lax.all_gather(projections, 'cls', axis=0, tiled=True)  15.3 us
    dot_general x4, matrix products, one_group(): lax.dot_general(ctf_square, magnitude.reshape(group_size * directions, pi...  9.16 us
    add x4, local copies, waits for them, and re-layouts, turn_refs(): second = real_ref[None] * sin_wide + imag_ref[None] * cos_wide  9.07 us
    dot_general x4, matrix products, one_group(): lax.dot_general(rows_in, turned.reshape(-1, 2 * pixel_count), (((1,), (1,...  8.57 us
    all_to_all x1, starting transfers between devices, per_device(): lax.all_to_all(send_codes, 'orient', split_axis=0, concat_axis=0, tiled=T...  6.35 us
  transfers between devices with their start and end apart: 6, of which 5 were waited for; matrix products, arithmetic and copies ran while one was open for 6% of the time, Pallas kernels for 0%

commit v1 on v0

--- a/solution.py
+++ b/solution.py
@@ -121,7 +121,12 @@
     )
     shift_total = cos_shift.shape[0]
     ctf_square = ctf_table * ctf_table
-    ref_piece = lax.all_gather(projections, "cls", axis=0, tiled=True)
+    ring = [projections]
+    for hop in range(3):
+        ring.append(lax.ppermute(ring[-1], "cls", [(dev, (dev + 1) % 4) for dev in range(4)]))
+    ref_piece = jnp.roll(
+        jnp.concatenate(ring[::-1], axis=0), (lax.axis_index("cls") + 1) * ring[0].shape[0], axis=0
+    )
     piece_rows = ref_piece.shape[0]
     group_size = 2
     grouped = ref_piece.reshape(piece_rows // group_size, group_size, directions, 2 * pixel_count)

time: 307 us -> 311 us (1.013)
  blocking collectives: 15.3 us -> 0 us
  waiting for transfers between devices: 131 us -> 145 us
  local copies, waits for them, and re-layouts: 44 us -> 49.4 us
  other arithmetic: 46.6 us -> 43.4 us
  starting transfers between devices: 21.8 us -> 25 us
    all_gather x1 -> x0, blocking collectives: 15.3 us -> none  [per_device(): ref_piece = lax.all_gather(projections, 'cls', axis=0, tiled=True)]
    all_to_all x1, waiting for transfers between devices: 74.1 us -> 87 us  [per_device(): lax.all_to_all(send_images, 'orient', split_axis=0, concat_axis=0, tiled=...]
    concatenate x0 -> x1, local copies, waits for them, and re-layouts: none -> 5.51 us  [per_device(): jnp.roll(jnp.concatenate(ring[::-1], axis=0), (lax.axis_index('cls') + 1)...]
    ppermute x0 -> x3, starting transfers between devices: none -> 5.15 us  [per_device(): lax.ppermute(ring[-1], 'cls', [(dev, (dev + 1) % 4) for dev in range(4)])]
    all_gather x1 -> x0, other arithmetic: 3.18 us -> none  [per_device(): ref_piece = lax.all_gather(projections, 'cls', axis=0, tiled=True)]
  transfers between devices with their start and end apart: 6 -> 9, of which waited for: 5 -> 6; matrix products, arithmetic and copies ran while one was open for 6% -> 7% of each run, Pallas kernels for 0% -> 0%
where the time goes in v1:
time: 311 us; the launch traced here: 310 us
  waiting for transfers between devices  145 us (47%)
  local copies, waits for them, and re-layouts  49.4 us (16%)
  other arithmetic  43.4 us (14%)
  matrix products  28.7 us (9%)
  starting transfers between devices  25 us (8%)
  between operations  14.9 us (5%)
    all_to_all x1, waiting for transfers between devices, per_device(): lax.all_to_all(send_images, 'orient', split_axis=0, concat_axis=0, tiled=...  87 us
    unnamed x2, waiting for transfers between devices  42.7 us
    cos x8, other arithmetic, rotation(): return (jnp.cos(angle), jnp.sin(angle))  24.6 us
    dot_general x4, matrix products, one_group(): lax.dot_general(ctf_square, magnitude.reshape(group_size * directions, pi...  9.16 us
    add x4, local copies, waits for them, and re-layouts, turn_refs(): second = real_ref[None] * sin_wide + imag_ref[None] * cos_wide  9.07 us
    dot_general x4, matrix products, one_group(): lax.dot_general(rows_in, turned.reshape(-1, 2 * pixel_count), (((1,), (1,...  8.57 us
  transfers between devices with their start and end apart: 9, of which 6 were waited for; matrix products, arithmetic and copies ran while one was open for 7% of the time, Pallas kernels for 0%

profile of v1, /device:TPU:0, one launch (start us, length us, event | category | flops | bytes accessed | tf_op | source)
XLA Modules:
  0.0 309.9 jit_solution(665000068920834455)
XLA Ops:
  7.2 3.0 collective-permute-start
  13.0 4.9 %all-to-all-start.1 = ((s32[8,1,6]{2,1,0:T(1,128)}), s32[8,1,6]{2,1,0:T(1,128)S(1)}, u32[]{:S(2)}, u32[]{:S(2)}) async-start(s32[8,1,6]{2,1,0:T(1,128)} %bitcast.3), calls=%async_computation.1 | async-start | bytes 8192 | tf_op jit(solution)/shard_map/all_to_all | solution.py:108
  19.3 6.1 %fusion.38 = (bf16[12,16512]{1,0:T(8,128)(2,1)S(1)}, bf16[12,16512]{1,0:T(8,128)(2,1)S(1)}) fusion(s32[12]{0:T(128)S(1)} %get-tuple-element.313, s32[16512]{0:T(1024)} %get-tuple-element.493, s32[12]{0:T(128)S(1)} %get-tuple-element.312, s32[16512]{0:T(1024)} %get-tuple-element.491, bf16[12,33024]{1,0:T(8,128)(2,1)} %param.12, bf16[8,16512]{1,0:T(8,128)(2,1)} %param.14, ...), kind=kOutput, calls=%fused_computation.63 | convolution fusion | flops 8718432 | bytes 1981584 | tf_op jit(solution)/shard_map/dot_general | solution.py:93
  25.5 1.5 collective-permute-start.1
  28.0 2.6 reshape.281
  30.6 1.7 collective-permute-done.1
  32.9 4.7 %all-to-all-start = ((bf16[8,6,33024]{2,1,0:T(8,128)(2,1)}), bf16[8,6,33024]{2,1,0:T(8,128)(2,1)}, u32[]{:S(2)}, u32[]{:S(2)}) async-start(bf16[8,6,33024]{2,1,0:T(8,128)(2,1)} %reshape.281), calls=%async_computation | async-start | bytes 8454144 | tf_op jit(solution)/shard_map/all_to_all | solution.py:107
  38.7 5.5 %concatenate.20 = bf16[16,1,33024]{2,0,1:T(8,128)(2,1)S(1)} concatenate(bf16[2,1,33024]{2,0,1:T(2,128)(2,1)S(1)} %collective-permute-done.2, bf16[2,1,33024]{2,0,1:T(2,128)(2,1)S(1)} %collective-permute-done.1, bf16[2,1,33024]{2,0,1:T(2,128)(2,1)S(1)} %collective-permute-done, bf16[2,1,33024]{2,0,1:T(2,128)(2,1)S(1)} %copy-done.2, ...), dimensions={0} | concatenate | bytes 2113536 | tf_op jit(solution)/shard_map/jit(_roll_dynamic)/concatenate | solution.py:127
  45.4 87.0 %all-to-all-done = bf16[8,6,33024]{2,1,0:T(8,128)(2,1)} async-done(((bf16[8,6,33024]{2,1,0:T(8,128)(2,1)}), bf16[8,6,33024]{2,1,0:T(8,128)(2,1)}, u32[]{:S(2)}, u32[]{:S(2)}) %all-to-all-start) | async-done | bytes 3170336 | tf_op jit(solution)/shard_map/all_to_all | solution.py:107
  132.4 2.8 reshape.282
  135.3 57.9 %while.24 = (s32[]{:T(128)}, f32[4,48,5,2,1]{1,3,2,4,0:T(2,128)S(1)}, bf16[4,2,1,33024]{3,1,2,0:T(2,128)(2,1)}, bf16[48,33024]{1,0:T(8,128)(2,1)S(1)}, f32[8,165...) while((s32[]{:T(128)}, ...), condition=%wide.region_5.6_spmd.clone.clone, body=%wide.region_4.5_spmd.clone.clone.sunk | while | flops 39077952 | bytes 9925141 | solution.py:155
  135.3 3.1 fusion.95
  140.0 1.4 subtract_convert_fusion.2
  141.5 2.3 add.667
  143.7 1.3 sub.147
  145.0 2.1 convolution_bitcast_fusion.5
  147.2 2.3 fusion.96
  149.8 3.1 fusion.95
  154.5 1.4 subtract_convert_fusion.2
  155.9 2.3 add.667
  158.2 1.3 sub.147
  159.5 2.1 convolution_bitcast_fusion.5
  161.7 2.3 fusion.96
  164.3 3.1 fusion.95
  169.0 1.4 subtract_convert_fusion.2
  170.4 2.3 add.667
  174.0 2.1 convolution_bitcast_fusion.5
  176.2 2.3 fusion.96
  178.7 3.1 fusion.95
  183.5 1.4 subtract_convert_fusion.2
  184.9 2.3 add.667
  187.2 1.3 sub.147
  188.5 2.1 convolution_bitcast_fusion.5
  190.7 2.3 fusion.96
  194.0 3.3 %all-to-all-start.3 = ((f32[8,1,6]{2,1,0:T(1,128)}), f32[8,1,6]{2,1,0:T(1,128)S(1)}, u32[]{:S(2)}, u32[]{:S(2)}) async-start(f32[8,1,6]{2,1,0:T(1,128)} %bitcast.8), calls=%async_computation.3 | async-start | bytes 8192 | tf_op jit(solution)/shard_map/all_to_all | solution.py:169
  198.1 4.7 %all-to-all-done.3 = f32[8,1,6]{2,1,0:T(1,128)S(1)} async-done(((f32[8,1,6]{2,1,0:T(1,128)}), f32[8,1,6]{2,1,0:T(1,128)S(1)}, u32[]{:S(2)}, u32[]{:S(2)}) %all-to-all-start.3) | async-done | bytes 224 | tf_op jit(solution)/shard_map/all_to_all | solution.py:169
  202.8 3.3 %all-to-all-start.2 = ((f32[8,1,6]{2,1,0:T(1,128)}), f32[8,1,6]{2,1,0:T(1,128)S(1)}, u32[]{:S(2)}, u32[]{:S(2)}) async-start(f32[8,1,6]{2,1,0:T(1,128)} %bitcast.4), calls=%async_computation.2 | async-start | bytes 8192 | tf_op jit(solution)/shard_map/all_to_all | solution.py:162
  207.4 4.2 %all-to-all-done.2 = f32[8,1,6]{2,1,0:T(1,128)S(1)} async-done(((f32[8,1,6]{2,1,0:T(1,128)}), f32[8,1,6]{2,1,0:T(1,128)S(1)}, u32[]{:S(2)}, u32[]{:S(2)}) %all-to-all-start.2) | async-done | bytes 224 | tf_op jit(solution)/shard_map/all_to_all | solution.py:162
  213.9 3.3 %all-to-all-start.4 = ((f32[8,1,6]{2,1,0:T(1,128)}), f32[8,1,6]{2,1,0:T(1,128)S(1)}, u32[]{:S(2)}, u32[]{:S(2)}) async-start(f32[8,1,6]{2,1,0:T(1,128)} %bitcast.13), calls=%async_computation.4 | async-start | bytes 8192 | tf_op jit(solution)/shard_map/all_to_all | solution.py:188
  217.6 5.0 %all-to-all-done.4 = f32[8,1,6]{2,1,0:T(1,128)S(1)} async-done(((f32[8,1,6]{2,1,0:T(1,128)}), f32[8,1,6]{2,1,0:T(1,128)S(1)}, u32[]{:S(2)}, u32[]{:S(2)}) %all-to-all-start.4) | async-done | bytes 224 | tf_op jit(solution)/shard_map/all_to_all | solution.py:188
  223.5 28.0 %while.25 = (s32[]{:T(128)}, bf16[4,2,1,33024]{3,2,1,0:T(2,128)(2,1)}, s32[4]{0:T(128)S(1)}, bf16[48,5,8,1]{0,2,1,3:T(8,128)(2,1)S(1)}, bf16[48,33024]{1,0:T(8,1...) while((s32[]{:T(128)}, ...), condition=%wide.region_13.14_spmd.clone.clone, body=%wide.region_10.13_spmd.clone.clone.sunk | while | flops 34543108 | bytes 8065315 | solution.py:209
  225.3 3.1 fusion.100
  232.3 3.1 fusion.100
  239.3 3.1 fusion.100
  246.3 3.1 fusion.100
  251.5 4.8 %convert_reduce_fusion = bf16[4,2,33024]{2,1,0:T(2,128)(2,1)S(1)} fusion(bf16[4,2,1,33024]{3,2,1,0:T(2,128)(2,1)} %get-tuple-element.82), kind=kLoop, calls=%fused_computation.73 | loop fusion | bytes 1056768 | tf_op jit(solution)/shard_map/convert_element_type | solution.py:214
  258.6 42.6 %all-reduce.3.cloned.1.call-done = bf16[8,1,33024]{2,0,1:T(8,128)(2,1)} async-done(((bf16[8,1,33024]{2,0,1:T(8,128)(2,1)}), bf16[8,1,33024]{2,0,1:T(8,128)(2,1)}) %all-reduce.3.cloned.1.call-update) | async-done | bytes 528400
  301.2 1.8 constant_dynamic-slice_fusion.1
  (138 shorter events, 37.8 us)
Async XLA Ops:
  7.2 18.3 %collective-permute-start = (bf16[2,1,33024]{2,0,1:T(2,128)(2,1)}, bf16[2,1,33024]{2,0,1:T(2,128)(2,1)S(1)}, u32[]{:S(2)}, u32[]{:S(2)}) collective-permute-start(bf16[2,1,33024]{2,0,1:T(2,128)(2,1)} %param.13), channel_id=1, source_target_pairs={{0,1},{1,2},{2,3},{3,0},{4,5},{5,6},{6,7},{7,4},{8,9},{9,10},{10,1... | collective-permute-start | bytes 396296 | tf_op jit(solution)/shard_map/ppermute | solution.py:126
  13.0 19.9 %all-to-all-start.1 = ((s32[8,1,6]{2,1,0:T(1,128)}), s32[8,1,6]{2,1,0:T(1,128)S(1)}, u32[]{:S(2)}, u32[]{:S(2)}) async-start(s32[8,1,6]{2,1,0:T(1,128)} %bitcast.3), calls=%async_computation.1 | async-start | bytes 8192 | tf_op jit(solution)/shard_map/all_to_all | solution.py:108
  25.5 6.9 %collective-permute-start.1 = (bf16[2,1,33024]{2,0,1:T(2,128)(2,1)S(1)}, bf16[2,1,33024]{2,0,1:T(2,128)(2,1)S(1)}, u32[]{:S(2)}, u32[]{:S(2)}) collective-permute-start(bf16[2,1,33024]{2,0,1:T(2,128)(2,1)S(1)} %collective-permute-done), channel_id=1, source_target_pairs={{0,1},{1,2},{2,3},{3,0},{4,5},{5,6},{6,7},{7,4},{8,9},{9,10},{10,1... | collective-permute-start | bytes 396296 | tf_op jit(solution)/shard_map/ppermute | solution.py:126
  30.6 7.1 %copy-start.3 = (bf16[8,16512]{1,0:T(8,128)(2,1)S(1)}, bf16[8,16512]{1,0:T(8,128)(2,1)}, u32[]{:S(2)}) copy-start(bf16[8,16512]{1,0:T(8,128)(2,1)} %param.14) | copy-start | bytes 792580
  30.6 8.1 %copy-start.2 = (bf16[2,1,33024]{2,0,1:T(2,128)(2,1)S(1)}, bf16[2,1,33024]{2,0,1:T(2,128)(2,1)}, u32[]{:S(2)}) copy-start(bf16[2,1,33024]{2,0,1:T(2,128)(2,1)} %param.13) | copy-start | bytes 396292
  32.3 6.3 %collective-permute-start.2 = (bf16[2,1,33024]{2,0,1:T(2,128)(2,1)S(1)}, bf16[2,1,33024]{2,0,1:T(2,128)(2,1)S(1)}, u32[]{:S(2)}, u32[]{:S(2)}) collective-permute-start(bf16[2,1,33024]{2,0,1:T(2,128)(2,1)S(1)} %collective-permute-done.1), channel_id=1, source_target_pairs={{0,1},{1,2},{2,3},{3,0},{4,5},{5,6},{6,7},{7,4},{8,9},{9,10},{10,1... | collective-permute-start | bytes 396296 | tf_op jit(solution)/shard_map/ppermute | solution.py:126
  32.9 99.5 %all-to-all-start = ((bf16[8,6,33024]{2,1,0:T(8,128)(2,1)}), bf16[8,6,33024]{2,1,0:T(8,128)(2,1)}, u32[]{:S(2)}, u32[]{:S(2)}) async-start(bf16[8,6,33024]{2,1,0:T(8,128)(2,1)} %reshape.281), calls=%async_computation | async-start | bytes 8454144 | tf_op jit(solution)/shard_map/all_to_all | solution.py:107
  45.4 89.9 %copy-start.4 = (s32[5]{0:T(128)S(1)}, s32[5]{0:T(128)}, u32[]{:S(2)}) copy-start(s32[5]{0:T(128)} %constant.123.clone) | copy-start | bytes 64
  45.4 89.9 %copy-start.5 = (s32[5]{0:T(128)S(1)}, s32[5]{0:T(128)}, u32[]{:S(2)}) copy-start(s32[5]{0:T(128)} %constant.124.clone) | copy-start | bytes 64
  139.4 0.7 copy-start
  145.0 2.2 copy-start.1
  153.9 0.7 copy-start
  159.5 2.2 copy-start.1
  168.4 0.7 copy-start
  174.0 2.2 copy-start.1
  182.8 0.7 copy-start
  188.5 2.2 copy-start.1
  194.0 8.9 %all-to-all-start.3 = ((f32[8,1,6]{2,1,0:T(1,128)}), f32[8,1,6]{2,1,0:T(1,128)S(1)}, u32[]{:S(2)}, u32[]{:S(2)}) async-start(f32[8,1,6]{2,1,0:T(1,128)} %bitcast.8), calls=%async_computation.3 | async-start | bytes 8192 | tf_op jit(solution)/shard_map/all_to_all | solution.py:169
  202.8 8.8 %all-to-all-start.2 = ((f32[8,1,6]{2,1,0:T(1,128)}), f32[8,1,6]{2,1,0:T(1,128)S(1)}, u32[]{:S(2)}, u32[]{:S(2)}) async-start(f32[8,1,6]{2,1,0:T(1,128)} %bitcast.4), calls=%async_computation.2 | async-start | bytes 8192 | tf_op jit(solution)/shard_map/all_to_all | solution.py:162
  213.1 10.4 %copy-start.6 = (f32[12]{0:T(128)}, f32[12]{0:T(128)S(1)}, u32[]{:S(2)}) copy-start(f32[12]{0:T(128)S(1)} %log_add_fusion) | copy-start | bytes 148
  213.9 8.8 %all-to-all-start.4 = ((f32[8,1,6]{2,1,0:T(1,128)}), f32[8,1,6]{2,1,0:T(1,128)S(1)}, u32[]{:S(2)}, u32[]{:S(2)}) async-start(f32[8,1,6]{2,1,0:T(1,128)} %bitcast.13), calls=%async_computation.4 | async-start | bytes 8192 | tf_op jit(solution)/shard_map/all_to_all | solution.py:188
  217.2 83.9 %all-reduce.3.cloned.1.call-start = ((), (), s32[]{:S(2)}) async-start(), calls=%async_computation.5 | async-start | bytes 1056768
  256.3 1.1 copy-start.7
Sparse Core Ops, SparseCore 0:
  257.4 43.7 all-reduce.2
